TPU v7x, 128 devices: a whole 4x4x4 slice. The times are simulated.
128 devices in a mesh: proj: 16 (over z_lo, y, core), row: 8 (over x, z_hi).
Axes of the slice: x: 4, y: 4, z: 4 (z_hi: 2, z_lo: 2; z = z_hi * 2 + z_lo), core: 2. Of those that a mesh axis runs over, the one named last changes fastest.
Arguments:
- projections: float32 [8192, 8, 1536], P('proj', 'row'), may hold values from -40000 to 40000
Outputs:
- gram: float32 [8192, 8192], P('proj', 'row')
All inputs are finite; a program needn't handle non-finite values.
Results may differ from a plain program's by a relative error of at most 0.0017.
Values may be sent and summed in bfloat16 or wider, within the bound.
A program may use at most 128 MiB of HBM per device.

v0:
```python
import math
import jax
import jax.numpy as jnp
from jax import lax
from jax.sharding import PartitionSpec as P


def per_device(projections):
    tile_rows, det_rows, columns = projections.shape
    entries = det_rows * lax.axis_size("row") * columns
    filtered = projections - jnp.mean(projections, axis=2, keepdims=True)
    energy = lax.psum(jnp.sum(filtered * filtered, axis=(1, 2)), "row")
    band_power = energy / entries
    normed = (
        filtered * lax.rsqrt(band_power + 1e-05)[:, None, None] * (1.0 / math.sqrt(entries))
    ).astype(jnp.bfloat16)
    flattened = normed.reshape(tile_rows, det_rows * columns)
    contract = (((1,), (1,)), ((), ()))
    product = lax.dot_general(
        flattened,
        lax.all_gather(flattened, "proj", axis=0, tiled=True),
        contract,
        preferred_element_type=jnp.float32,
    )
    return lax.psum_scatter(product, "row", scatter_dimension=1, tiled=True)


def solution(mesh):
    in_specs = (P("proj", "row", None),)
    out_specs = P("proj", "row")
    return jax.shard_map(
        per_device, mesh=mesh, in_specs=in_specs, out_specs=out_specs, check_vma=False
    )
```

profile of v0, /device:TPU:0, one launch (start us, length us, event | category | flops | bytes accessed | tf_op | source)
XLA Modules:
  0.0 388.9 jit_solution(17753626626749477230)
XLA Ops:
  6.5 0.0 copy-start
  6.5 0.0 all-gather.3.cloned.1.call-start
  6.5 4.2 %reduce_sum.18 = f32[512]{0:T(512)S(1)} reduce(f32[512,1,1536]{2,1,0:T(1,128)} %param.1, f32[]{:T(128)} %constant.2.clone.1), dimensions={1,2}, to_apply=%region_0.0 | reduce | flops 785920 | bytes 3147780 | tf_op jit(solution)/shard_map/reduce_sum | solution.py:11
  10.8 0.0 copy-done
  10.8 0.4 multiply_reduce_fusion
  11.3 25.1 %psum.7 = f32[512]{0:T(512)S(1)} all-reduce(f32[512]{0:T(512)S(1)} %multiply_reduce_fusion), channel_id=1, replica_groups=mesh['proj'=16,'row'=8] {'row'}, use_global_device_ids=true, to_apply=%region_2.0 | all-reduce | flops 512 | bytes 4096 | tf_op jit(solution)/shard_map/psum | solution.py:12
  36.4 1.6 multiply_convert_fusion
  38.0 0.0 all-gather.3.cloned.1.call-update
  38.0 0.0 reduce-scatter.2.cloned.1.call-start
  38.1 128.1 %all-gather.3.cloned.1.call-done = bf16[8192,1,1536]{2,0,1:T(8,128)(2,1)} async-done(((bf16[512,1,1536]{2,0,1:T(8,128)(2,1)}), bf16[8192,1,1536]{2,0,1:T(8,128)(2,1)}) %all-gather.3.cloned.1.call-update) | async-done | bytes 25165840 | tf_op jit(solution)/shard_map/all_gather | solution.py:21
  166.2 20.8 %fusion = f32[512,8192]{1,0:T(8,128)} fusion(bf16[8192,1,1536]{2,0,1:T(8,128)(2,1)} %all-gather.3.cloned.1.call-done, bf16[512,1,1536]{2,0,1:T(8,128)(2,1)} %multiply_convert_fusion), kind=kOutput, calls=%fused_computation | convolution fusion | flops 12884901888 | bytes 43515904 | tf_op jit(solution)/shard_map/dot_general | solution.py:19
  187.0 0.0 reduce-scatter.2.cloned.1.call-update
  187.1 195.0 %reduce-scatter.2.cloned.1.call-done = f32[512,1024]{1,0:T(8,128)} async-done(((f32[512,8192]{1,0:T(8,128)}), f32[512,1024]{1,0:T(8,128)}) %reduce-scatter.2.cloned.1.call-update) | async-done | bytes 2097168 | tf_op jit(solution)/shard_map/reduce_scatter | solution.py:25
  (2 shorter events, 0.0 us)
Async XLA Ops:
  6.5 4.3 %copy-start = (f32[512,1,1536]{2,1,0:T(1,128)S(1)}, f32[512,1,1536]{2,1,0:T(1,128)}, u32[]{:S(2)}) copy-start(f32[512,1,1536]{2,1,0:T(1,128)} %param.1) | copy-start | bytes 9437188
  6.5 159.7 %all-gather.3.cloned.1.call-start = ((), (), s32[]{:S(2)}) async-start(), calls=%async_computation.2 | async-start | bytes 26738688 | tf_op jit(solution)/shard_map/all_gather | solution.py:21
  38.0 344.1 %reduce-scatter.2.cloned.1.call-start = ((), (), s32[]{:S(2)}) async-start(), calls=%async_computation.1 | async-start | bytes 18874368 | tf_op jit(solution)/shard_map/reduce_scatter | solution.py:25
Sparse Core Ops, SparseCore 0:
  38.2 127.9 all-gather.2
  187.2 194.8 reduce-scatter.1
where the time goes:
time: 389 us
  waiting for transfers between devices  323 us (83%)
  blocking collectives  25.1 us (6%)
  matrix products  20.8 us (5%)
  between operations  13.4 us (3%)
  other arithmetic  6.33 us (2%)
    reduce_scatter x1, waiting for transfers between devices, per_device(): return lax.psum_scatter(product, 'row', scatter_dimension=1, tiled=True)  195 us
    all_gather x1, waiting for transfers between devices, per_device(): lax.all_gather(flattened, 'proj', axis=0, tiled=True)  128 us
    psum x1, blocking collectives, per_device(): energy = lax.psum(jnp.sum(filtered * filtered, axis=(1, 2)), 'row')  25.1 us
    dot_general x1, matrix products, per_device(): lax.dot_general(flattened, lax.all_gather(flattened, 'proj', axis=0, tile...  20.8 us
  transfers between devices with their start and end apart: 2, of which 2 were waited for; matrix products, arithmetic and copies ran while one was open for 0% of the time, Pallas kernels for 0%

commit v1 on v0

--- a/solution.py
+++ b/solution.py
@@ -18,7 +18,12 @@
     contract = (((1,), (1,)), ((), ()))
     product = lax.dot_general(
         flattened,
-        lax.all_gather(flattened, "proj", axis=0, tiled=True),
+        jnp.concatenate(
+            jax.lax.all_to_all(
+                jnp.stack([flattened for _ in range(jax.lax.psum(1, "proj"))]), "proj", 0, 0
+            ),
+            axis=0,
+        ),
         contract,
         preferred_element_type=jnp.float32,
     )

time: 389 us -> 543 us (1.40)
  blocking collectives: 25.1 us -> 305 us
  waiting for transfers between devices: 323 us -> 188 us
  other arithmetic: 6.33 us -> 12.9 us
    all_to_all x0 -> x1, blocking collectives: none -> 280 us  [per_device(): jax.lax.all_to_all(jnp.stack([flattened for _ in range(jax.lax.psum(1, 'p...]
    all_gather x1 -> x0, waiting for transfers between devices: 128 us -> none  [per_device(): lax.all_gather(flattened, 'proj', axis=0, tiled=True)]
    reduce_scatter x1, waiting for transfers between devices: 195 us -> 188 us  [per_device(): return lax.psum_scatter(product, 'row', scatter_dimension=1, tiled=True)]
  transfers between devices with their start and end apart: 2 -> 1, of which waited for: 2 -> 1; matrix products, arithmetic and copies ran while one was open for 0% -> 0% of each run, Pallas kernels for 0% -> 0%
where the time goes in v1:
time: 543 us
  blocking collectives  305 us (56%)
  waiting for transfers between devices  188 us (35%)
  matrix products  20.4 us (4%)
  between operations  13.4 us (2%)
  other arithmetic  12.9 us (2%)
    all_to_all x1, blocking collectives, per_device(): jax.lax.all_to_all(jnp.stack([flattened for _ in range(jax.lax.psum(1, 'p...  280 us
    reduce_scatter x1, waiting for transfers between devices, per_device(): return lax.psum_scatter(product, 'row', scatter_dimension=1, tiled=True)  188 us
    psum x1, blocking collectives, per_device(): energy = lax.psum(jnp.sum(filtered * filtered, axis=(1, 2)), 'row')  25.1 us
    dot_general x1, matrix products, per_device(): lax.dot_general(flattened, jnp.concatenate(jax.lax.all_to_all(jnp.stack([...  20.4 us
  transfers between devices with their start and end apart: 1, of which 1 were waited for; matrix products, arithmetic and copies ran while one was open for 0% of the time, Pallas kernels for 0%

profile of v1, /device:TPU:0, one launch (start us, length us, event | category | flops | bytes accessed | tf_op | source)
XLA Modules:
  0.0 542.8 jit_solution(8581784884207246084)
XLA Ops:
  6.5 0.0 copy-start
  6.5 0.0 reduce-scatter.2.cloned.1.call-start
  6.5 4.2 reduce_sum.18
  10.8 0.0 copy-done
  10.8 3.9 multiply_reduce_fusion
  14.7 25.1 %psum.7 = f32[512]{0:T(512)S(1)} all-reduce(f32[512]{0:T(512)S(1)} %multiply_reduce_fusion), channel_id=1, replica_groups=mesh['proj'=16,'row'=8] {'row'}, use_global_device_ids=true, to_apply=%region_2.0 | all-reduce | flops 512 | bytes 4096 | tf_op jit(solution)/shard_map/psum | solution.py:12
  39.9 4.7 multiply_convert_fusion
  44.6 0.3 copy.4
  44.9 2.6 stack.3
  47.5 279.8 %all_to_all.5 = bf16[16,512,1536]{2,1,0:T(8,128)(2,1)} all-to-all(bf16[16,512,1536]{2,1,0:T(8,128)(2,1)S(1)} %stack.3), channel_id=1, replica_groups=mesh['proj'=16,'row'=8] {'proj'}, dimensions={0} | all-to-all | bytes 50331648 | tf_op jit(solution)/shard_map/all_to_all | solution.py:22
  327.3 20.4 %fusion = f32[512,8192]{1,0:T(8,128)} fusion(bf16[512,1536]{1,0:T(8,128)(2,1)S(1)} %bitcast.8, bf16[8192,1536]{1,0:T(8,128)(2,1)} %bitcast.6), kind=kOutput, calls=%fused_computation.5 | convolution fusion | flops 12884901888 | bytes 43515904 | tf_op jit(solution)/shard_map/dot_general | solution.py:19
  347.7 0.0 reduce-scatter.2.cloned.1.call-update
  347.7 188.3 %reduce-scatter.2.cloned.1.call-done = f32[512,1024]{1,0:T(8,128)} async-done(((f32[512,8192]{1,0:T(8,128)}), f32[512,1024]{1,0:T(8,128)}) %reduce-scatter.2.cloned.1.call-update) | async-done | bytes 2097168 | tf_op jit(solution)/shard_map/reduce_scatter | solution.py:30
  (2 shorter events, 0.0 us)
Async XLA Ops:
  6.5 4.3 copy-start
  6.5 529.4 %reduce-scatter.2.cloned.1.call-start = ((), (), s32[]{:S(2)}) async-start(), calls=%async_computation.2 | async-start | bytes 18874368 | tf_op jit(solution)/shard_map/reduce_scatter | solution.py:30
Sparse Core Ops, SparseCore 0:
  347.8 188.0 reduce-scatter.1
